TPU v7x, 256 devices: a whole 4x4x8 slice. The times are simulated.
256 devices in a mesh: pts: 8 (over x, core), rows: 32 (over z, y).
Axes of the slice: x: 4, y: 4, z: 8, core: 2. Of those that a mesh axis runs over, the one named last changes fastest.
Arguments:
- solutions: bfloat16 [16, 262144, 128], P('pts', 'rows'), may hold values from -6 to 6
- probe: bfloat16 [64, 262144], P(None, 'rows'), may hold values from -0.01171875 to 0.01171875
- left_factor: float32 [256, 256], replicated, may hold values from -0.375 to 0.375
- singular: float32 [256], replicated, may hold values from 1 to 13.8, as said below
- right_factor: float32 [256, 256], replicated, may hold values from -0.375 to 0.375
- reduced_adjoint: float32 [256, 256], replicated, may hold values from -6 to 6
Outputs:
- solution_adjoint: bfloat16 [16, 262144, 128], P('pts', 'rows')
Inputs may be any that keep to these rules, and one draw needn't show every extreme that they name: `singular`: rising, each value at least 0.03 above the one before.
All inputs are finite; a program needn't handle non-finite values.
Results may differ from a plain program's by a relative error of at most 0.0049.
Values sent between devices are 32-bit elements; how exact they have to be, the bound alone decides.
A program may use at most 64 MiB of HBM per device.

v0:
```python
import math
import jax
import jax.numpy as jnp
from jax import lax
from jax.sharding import PartitionSpec as P

L = 64
K = 4


def coefficients(first, count, total, orders):
    theta = math.pi * (first + jnp.arange(count, dtype=jnp.float32) + 0.5) / total
    angle = theta[:, None] * orders[None, :]
    return (jnp.cos(angle) / total, jnp.sin(angle) / total)


def matmul(first, second):
    return jnp.dot(
        first, second, precision=lax.Precision.HIGHEST, preferred_element_type=jnp.float32
    )


def svd_back(hankel, left, sing, right, adjoint):
    quot = matmul(left.T, hankel)
    prod_right = matmul(hankel, right)
    zmat = matmul(quot, right)
    zbar = adjoint / sing[None, :]
    sbar = -jnp.sum(adjoint * zmat, axis=0) / (sing * sing)
    ubar = matmul(prod_right, zbar.T)
    wbar = matmul(quot.T, zbar)
    left_term = matmul(left.T, ubar)
    right_term = matmul(right.T, wbar)
    square = sing * sing
    eye_mask = jnp.eye(sing.shape[0], dtype=bool)
    recip = jnp.where(
        eye_mask, 0.0, 1.0 / jnp.where(eye_mask, 1.0, square[None, :] - square[:, None])
    )
    core = (
        recip * (left_term - left_term.T) * sing[None, :]
        + jnp.diag(sbar)
        + sing[:, None] * (recip * (right_term - right_term.T))
    )
    return (core, zbar)


def build_hankel(moments):
    return jnp.concatenate(
        [jnp.concatenate([moments[i + j] for j in range(K)], axis=1) for i in range(K)], axis=0
    )


def per_device(solutions, probe, left_factor, singular, right_factor, reduced_adjoint):
    hi = lax.Precision.HIGHEST
    point_count = solutions.shape[0]
    total = point_count * lax.axis_size("pts")
    first = (lax.axis_index("pts") * point_count).astype(jnp.float32)
    orders = jnp.arange(1, 2 * K + 1, dtype=jnp.float32)
    cos_t, sin_t = coefficients(first, point_count, total, orders)
    gram = jnp.einsum("ln,pnc->plc", probe, solutions, preferred_element_type=jnp.float32)
    moments = lax.psum(
        jnp.einsum("pk,plc->klc", cos_t[:, 1:], gram[:, :, :L], precision=hi)
        - jnp.einsum("pk,plc->klc", sin_t[:, 1:], gram[:, :, L:], precision=hi),
        ("pts", "rows"),
    )
    hankel = build_hankel(moments)
    core, zbar = svd_back(hankel, left_factor, singular, right_factor, reduced_adjoint)
    first_bar = matmul(matmul(left_factor, core), right_factor.T)
    second_bar = matmul(matmul(left_factor, zbar), right_factor.T)
    blocks = [jnp.zeros((L, L), jnp.float32) for k in range(2 * K)]
    for i in range(K):
        for j in range(K):
            blocks[i + j] = blocks[i + j] + first_bar[i * L : (i + 1) * L, j * L : (j + 1) * L]
            blocks[i + j + 1] = (
                blocks[i + j + 1] + second_bar[i * L : (i + 1) * L, j * L : (j + 1) * L]
            )
    moment_adjoint = jnp.stack(blocks)
    weights = jnp.concatenate(
        [
            jnp.einsum("pk,klc->plc", cos_t, moment_adjoint, precision=hi),
            -jnp.einsum("pk,klc->plc", sin_t, moment_adjoint, precision=hi),
        ],
        axis=2,
    ).astype(jnp.bfloat16)
    result = jnp.einsum("ln,plc->pnc", probe, weights, preferred_element_type=jnp.float32)
    return result.astype(jnp.bfloat16)


def solution(mesh):
    in_specs = (P("pts", "rows", None), P(None, "rows"), P(), P(), P(), P())
    out_specs = P("pts", "rows", None)
    return jax.shard_map(
        per_device, mesh=mesh, in_specs=in_specs, out_specs=out_specs, check_vma=False
    )
```

profile of v0, /device:TPU:2, one launch (start us, length us, event | category | flops | bytes accessed | tf_op | source)
XLA Modules:
  0.0 296.1 jit_solution(6354948563807823471)
XLA Ops:
  6.6 1.1 copy-done
  7.8 3.0 %convolution_bitcast_fusion = f32[2,64,128]{2,1,0:T(8,128)S(1)} fusion(bf16[2,8192,128]{2,1,0:T(8,128)(2,1)} %param.6, bf16[64,8192]{1,0:T(8,128)(2,1)S(1)} %copy-done), kind=kOutput, calls=%fused_computation.5 | convolution fusion | flops 268435456 | bytes 5308416 | tf_op jit(solution)/shard_map/ln,pnc->plc/dot_general | solution.py:59
  10.7 0.1 fusion.69
  10.8 0.1 fusion.51
  10.9 0.5 fusion.31
  11.5 1.2 convolution_subtract_fusion
  12.7 0.6 fusion.63
  13.3 0.6 fusion.73
  13.9 256.3 %all-reduce.2.cloned.1.call-done = f32[7,64,64]{2,0,1:T(8,128)} async-done(((f32[7,64,64]{2,0,1:T(8,128)}), f32[7,64,64]{2,0,1:T(8,128)}) %all-reduce.2.cloned.1.call-update) | async-done | bytes 114704 | tf_op jit(solution)/shard_map/psum | solution.py:60
  270.3 2.1 fusion.68
  272.4 0.7 fusion.66
  273.1 0.6 fusion.1
  273.7 0.4 fusion.64
  274.1 0.4 fusion.67
  274.6 0.6 fusion.71
  275.2 0.4 fusion.65
  275.6 0.6 fusion.70
  276.2 0.1 copy.15
  276.4 0.1 copy.16
  276.5 0.7 fusion.7
  277.3 0.6 fusion.72
  277.9 0.1 fusion.45
  277.9 0.1 fusion.43
  278.0 0.1 fusion.41
  278.1 0.1 fusion.39
  278.2 0.1 fusion.37
  278.3 0.1 fusion.35
  278.4 0.1 fusion.33
  278.5 0.5 fusion.20
  279.0 0.5 fusion.18
  279.6 3.3 %fusion = bf16[2,8192,128]{1,2,0:T(8,128)(2,1)} fusion(bf16[64,8192]{1,0:T(8,128)(2,1)S(1)} %copy-done, bf16[2,64,64]{2,1,0:T(8,128)(2,1)S(1)} %fusion.29, bf16[2,64,64]{2,1,0:T(8,128)(2,1)S(1)} %copy.39), kind=kOutput, calls=%fused_computation.1 | convolution fusion | flops 270598144 | bytes 5275648 | tf_op jit(solution)/shard_map/ln,plc->pnc/dot_general | solution.py:84
  282.9 6.3 %copy.17 = bf16[2,8192,128]{2,1,0:T(8,128)(2,1)} copy(bf16[2,8192,128]{1,2,0:T(8,128)(2,1)} %fusion) | data formatting | bytes 8388608 | tf_op jit(solution)/shard_map/convert_element_type | solution.py:85
  (17 shorter events, 0.1 us)
Async XLA Ops:
  6.5 1.2 copy-start
  6.5 6.2 %copy-start.4 = (f32[256]{0:T(256)S(1)}, f32[256]{0:T(256)}, u32[]{:S(2)}) copy-start(f32[256]{0:T(256)} %param.9) | copy-start | bytes 3076
  6.5 6.2 %copy-start.3 = (f32[256,256]{1,0:T(8,128)S(1)}, f32[256,256]{1,0:T(8,128)}, u32[]{:S(2)}) copy-start(f32[256,256]{1,0:T(8,128)} %param.11) | copy-start | bytes 786436
  6.5 6.2 %copy-start.2 = (f32[256,256]{1,0:T(8,128)S(1)}, f32[256,256]{1,0:T(8,128)}, u32[]{:S(2)}) copy-start(f32[256,256]{1,0:T(8,128)} %param.8) | copy-start | bytes 786436
  6.5 6.8 %copy-start.1 = (f32[256,256]{1,0:T(8,128)S(1)}, f32[256,256]{1,0:T(8,128)}, u32[]{:S(2)}) copy-start(f32[256,256]{1,0:T(8,128)} %param.10) | copy-start | bytes 786436
  6.5 263.7 %all-reduce.2.cloned.1.call-start = ((), (), s32[]{:S(2)}) async-start(), calls=%async_computation | async-start | bytes 524288 | tf_op jit(solution)/shard_map/psum | solution.py:60
Sparse Core Ops, SparseCore 0:
  12.8 257.4 all-reduce.1
where the time goes:
time: 296 us
  waiting for transfers between devices  256 us (86%)
  matrix products  15.4 us (5%)
  between operations  13.7 us (5%)
  local copies, waits for them, and re-layouts  9.97 us (3%)
    psum x1, waiting for transfers between devices, per_device(): lax.psum(jnp.einsum('pk,plc->klc', cos_t[:, 1:], gram[:, :, :L], precisio...  256 us
    dot_general x11, matrix products, matmul(): jnp.dot(first, second, precision=lax.Precision.HIGHEST, preferred_element...  6.33 us
    convert_element_type x1, local copies, waits for them, and re-layouts, per_device(): return result.astype(jnp.bfloat16)  6.31 us
  transfers between devices with their start and end apart: 1, of which 1 were waited for; matrix products, arithmetic and copies ran while one was open for 0% of the time, Pallas kernels for 0%

commit v1 on v0

--- a/solution.py
+++ b/solution.py
@@ -58,9 +58,12 @@
     cos_t, sin_t = coefficients(first, point_count, total, orders)
     gram = jnp.einsum("ln,pnc->plc", probe, solutions, preferred_element_type=jnp.float32)
     moments = lax.psum(
-        jnp.einsum("pk,plc->klc", cos_t[:, 1:], gram[:, :, :L], precision=hi)
-        - jnp.einsum("pk,plc->klc", sin_t[:, 1:], gram[:, :, L:], precision=hi),
-        ("pts", "rows"),
+        lax.psum(
+            jnp.einsum("pk,plc->klc", cos_t[:, 1:], gram[:, :, :L], precision=hi)
+            - jnp.einsum("pk,plc->klc", sin_t[:, 1:], gram[:, :, L:], precision=hi),
+            "pts",
+        ),
+        "rows",
     )
     hankel = build_hankel(moments)
     core, zbar = svd_back(hankel, left_factor, singular, right_factor, reduced_adjoint)

time: 296 us -> 256 us (0.86)
  waiting for transfers between devices: 256 us -> 216 us
    psum x1, waiting for transfers between devices: 256 us -> 65.6 us  [per_device(): lax.psum(jnp.einsum('pk,plc->klc', cos_t[:, 1:], gram[:, :, :L], precisio...]
    psum x0 -> x1, waiting for transfers between devices: none -> 150 us  [per_device(): lax.psum(lax.psum(jnp.einsum('pk,plc->klc', cos_t[:, 1:], gram[:, :, :L],...]
  transfers between devices with their start and end apart: 1 -> 2, of which waited for: 1 -> 2; matrix products, arithmetic and copies ran while one was open for 0% -> 0% of each run, Pallas kernels for 0% -> 0%
where the time goes in v1:
time: 256 us; the launch traced here: 255 us
  waiting for transfers between devices  216 us (84%)
  matrix products  15.4 us (6%)
  between operations  13.7 us (5%)
  local copies, waits for them, and re-layouts  10.1 us (4%)
    psum x1, waiting for transfers between devices, per_device(): lax.psum(lax.psum(jnp.einsum('pk,plc->klc', cos_t[:, 1:], gram[:, :, :L],...  150 us
    psum x1, waiting for transfers between devices, per_device(): lax.psum(jnp.einsum('pk,plc->klc', cos_t[:, 1:], gram[:, :, :L], precisio...  65.6 us
    dot_general x11, matrix products, matmul(): jnp.dot(first, second, precision=lax.Precision.HIGHEST, preferred_element...  6.32 us
    convert_element_type x1, local copies, waits for them, and re-layouts, per_device(): return result.astype(jnp.bfloat16)  6.31 us
  transfers between devices with their start and end apart: 2, of which 2 were waited for; matrix products, arithmetic and copies ran while one was open for 0% of the time, Pallas kernels for 0%

profile of v1, /device:TPU:2, one launch (start us, length us, event | category | flops | bytes accessed | tf_op | source)
XLA Modules:
  0.0 255.4 jit_solution(12980207501158944608)
XLA Ops:
  6.6 1.1 copy-done
  7.8 3.0 %convolution_bitcast_fusion = f32[2,64,128]{2,1,0:T(8,128)S(1)} fusion(bf16[2,8192,128]{2,1,0:T(8,128)(2,1)} %param.6, bf16[64,8192]{1,0:T(8,128)(2,1)S(1)} %copy-done), kind=kOutput, calls=%fused_computation.5 | convolution fusion | flops 268435456 | bytes 5308416 | tf_op jit(solution)/shard_map/ln,pnc->plc/dot_general | solution.py:59
  10.7 0.1 fusion.69
  10.8 0.1 fusion.51
  10.9 0.5 fusion.31
  11.5 1.2 convolution_subtract_fusion
  12.8 0.6 fusion.63
  13.4 65.6 %all-reduce.3.cloned.1.call-done = f32[7,64,64]{2,0,1:T(8,128)} async-done(((f32[7,64,64]{2,0,1:T(8,128)}), f32[7,64,64]{2,0,1:T(8,128)}) %all-reduce.3.cloned.1.call-update) | async-done | bytes 114704 | tf_op jit(solution)/shard_map/psum | solution.py:61
  79.0 0.6 fusion.73
  79.6 149.9 %all-reduce.5.cloned.1.call-done = f32[7,64,64]{2,0,1:T(8,128)} async-done(((f32[7,64,64]{2,0,1:T(8,128)}), f32[7,64,64]{2,0,1:T(8,128)}) %all-reduce.5.cloned.1.call-update) | async-done | bytes 114704 | tf_op jit(solution)/shard_map/psum | solution.py:60
  229.5 2.2 fusion.68
  231.7 0.7 fusion.66
  232.4 0.6 fusion.1
  233.0 0.4 fusion.64
  233.4 0.4 fusion.67
  233.9 0.6 fusion.71
  234.5 0.4 fusion.65
  234.9 0.6 fusion.70
  235.5 0.1 copy.15
  235.7 0.1 copy.16
  235.8 0.7 fusion.7
  236.6 0.6 fusion.72
  237.2 0.1 fusion.45
  237.3 0.1 fusion.43
  237.4 0.1 fusion.41
  237.5 0.1 fusion.39
  237.6 0.1 fusion.37
  237.7 0.1 fusion.35
  237.8 0.5 fusion.20
  238.4 0.5 fusion.18
  238.9 3.3 %fusion = bf16[2,8192,128]{1,2,0:T(8,128)(2,1)} fusion(bf16[64,8192]{1,0:T(8,128)(2,1)S(1)} %copy-done, bf16[2,64,64]{2,1,0:T(8,128)(2,1)S(1)} %fusion.29, bf16[2,64,64]{2,1,0:T(8,128)(2,1)S(1)} %copy.39), kind=kOutput, calls=%fused_computation.1 | convolution fusion | flops 270598144 | bytes 5275648 | tf_op jit(solution)/shard_map/ln,plc->pnc/dot_general | solution.py:87
  242.2 6.3 %copy.17 = bf16[2,8192,128]{2,1,0:T(8,128)(2,1)} copy(bf16[2,8192,128]{1,2,0:T(8,128)(2,1)} %fusion) | data formatting | bytes 8388608 | tf_op jit(solution)/shard_map/convert_element_type | solution.py:88
  (20 shorter events, 0.2 us)
Async XLA Ops:
  6.5 1.2 copy-start
  6.5 6.2 %copy-start.4 = (f32[256]{0:T(256)S(1)}, f32[256]{0:T(256)}, u32[]{:S(2)}) copy-start(f32[256]{0:T(256)} %param.9) | copy-start | bytes 3076
  6.5 6.2 %copy-start.3 = (f32[256,256]{1,0:T(8,128)S(1)}, f32[256,256]{1,0:T(8,128)}, u32[]{:S(2)}) copy-start(f32[256,256]{1,0:T(8,128)} %param.11) | copy-start | bytes 786436
  6.5 6.2 %copy-start.2 = (f32[256,256]{1,0:T(8,128)S(1)}, f32[256,256]{1,0:T(8,128)}, u32[]{:S(2)}) copy-start(f32[256,256]{1,0:T(8,128)} %param.8) | copy-start | bytes 786436
  6.5 72.4 %copy-start.1 = (f32[256,256]{1,0:T(8,128)S(1)}, f32[256,256]{1,0:T(8,128)}, u32[]{:S(2)}) copy-start(f32[256,256]{1,0:T(8,128)} %param.10) | copy-start | bytes 786436
  6.5 72.4 %all-reduce.3.cloned.1.call-start = ((), (), s32[]{:S(2)}) async-start(), calls=%async_computation | async-start | bytes 524288 | tf_op jit(solution)/shard_map/psum | solution.py:61
  12.7 216.8 %all-reduce.5.cloned.1.call-start = ((), (), s32[]{:S(2)}) async-start(), calls=%async_computation.1 | async-start | bytes 524288 | tf_op jit(solution)/shard_map/psum | solution.py:60
Sparse Core Ops, SparseCore 0:
  12.8 66.1 all-reduce.2
  82.4 147.0 all-reduce.4
